TPU v7x, 128 devices: a whole 4x4x4 slice. The times are simulated.
128 devices in a mesh: pr: 16 (over z, x), pc: 8 (over y, core).
Axes of the slice: x: 4, y: 4, z: 4, core: 2. Of those that a mesh axis runs over, the one named last changes fastest.
Arguments:
- trailing: float32 [20480, 20480], P('pr', 'pc'), may hold values from -25 to 25, as said below
- v_panels: float32 [6, 32, 20480], P(None, None, ('pr', 'pc')), may hold values from -0.078125 to 0.078125
- t_panels: float32 [6, 32, 32], replicated, may hold values from -0.2 to 0.5, as said below
Outputs:
- updated: float32 [20480, 20480], P('pr', 'pc')
- w_panels: float32 [6, 32, 20480], P(None, None, ('pr', 'pc'))
Inputs may be any that keep to these rules, and one draw needn't show every extreme that they name: trailing is exactly symmetric. `t_panels`: each panel's factor is upper triangular with diagonal entries of 0.25 to 0.5.
All inputs are finite; a program needn't handle non-finite values.
Results may differ from a plain program's by a relative error of at most 0.00013.
Values sent between devices are 32-bit elements; how exact they have to be, the bound alone decides.
A program may use at most 128 MiB of HBM per device.

v0:
```python
import jax
import jax.numpy as jnp
from jax import lax
from jax.sharding import PartitionSpec as P


def broadcast(value, axis, source):
    kept = jnp.where(lax.axis_index(axis) == source, value, 0).astype(value.dtype)
    return lax.psum(kept, axis)


def contract(left_side, right_side, left_dim, right_dim):
    return lax.dot_general(
        left_side,
        right_side,
        (((left_dim,), (right_dim,)), ((), ())),
        precision=lax.Precision.HIGHEST,
        preferred_element_type=jnp.float32,
    )


def fetch_v_columns(v_row, col_rank, ratio):
    pieces = []
    for offset in range(ratio):
        pieces.append(broadcast(v_row, "pr", col_rank * ratio + offset))
    return jnp.concatenate(pieces, axis=1)


def fetch_w_columns(w_row, col_rank, ratio):
    pieces = []
    for offset in range(ratio):
        pieces.append(broadcast(w_row, "pr", col_rank * ratio + offset))
    return jnp.concatenate(pieces, axis=1)


def per_device(trailing, v_panels, t_panels):
    matrix = trailing
    rows_here = matrix.shape[0]
    col_rank = lax.axis_index("pc")
    ratio = lax.axis_size("pr") // lax.axis_size("pc")
    share = rows_here // lax.axis_size("pc")
    w_blocks = []
    for panel in range(v_panels.shape[0]):
        v_row = lax.all_gather(v_panels[panel], "pc", axis=1, tiled=True)
        v_col = fetch_v_columns(v_row, col_rank, ratio)
        factor = t_panels[panel]
        partial_value = contract(v_col, matrix, 1, 1)
        x_row = lax.psum(partial_value, "pc")
        gram_block = lax.psum(contract(v_row, x_row, 1, 1), "pr")
        middle = contract(contract(factor, gram_block, 0, 0), factor, 1, 0)
        w_row = contract(factor, x_row, 0, 0) - 0.5 * contract(middle, v_row, 0, 0)
        w_col = fetch_w_columns(w_row, col_rank, ratio)
        left_side = jnp.concatenate([v_row, w_row], axis=0)
        right_side = jnp.concatenate([w_col, v_col], axis=0)
        matrix = matrix - contract(left_side, right_side, 0, 0)
        w_blocks.append(lax.dynamic_slice_in_dim(w_row, col_rank * share, share, 1))
    return (matrix, jnp.stack(w_blocks))


def solution(mesh):
    return jax.shard_map(
        per_device,
        mesh=mesh,
        in_specs=(P("pr", "pc"), P(None, None, ("pr", "pc")), P()),
        out_specs=(P("pr", "pc"), P(None, None, ("pr", "pc"))),
        check_vma=False,
    )
```

profile of v0, /device:TPU:0, one launch (start us, length us, event | category | flops | bytes accessed | tf_op | source)
XLA Modules:
  0.0 1610.5 jit_solution(2257900202977496059)
XLA Ops:
  8.2 13.8 all-gather
  23.3 13.2 all-gather.1
  36.9 71.9 %all-reduce.45.cloned.1.call-done = (f32[32,1280]{1,0:T(8,128)}, f32[32,1280]{1,0:T(8,128)}) async-done(((f32[32,1280]{1,0:T(8,128)}, f32[32,1280]{1,0:T(8,128)}), (f32[32,1280]{1,0:T(8,128)}, f32[32,1280]{1,0:T(8,128)})) %all-reduce.45.cloned.1.call-update) | async-done | bytes 327696 | tf_op jit(solution)/shard_map/psum | solution.py:9
  110.6 15.3 fusion.109
  126.8 56.5 %all-reduce.21.cloned.1.call-done = f32[32,1280]{1,0:T(8,128)} async-done(((f32[32,1280]{1,0:T(8,128)}), f32[32,1280]{1,0:T(8,128)}) %all-reduce.21.cloned.1.call-update) | async-done | bytes 163856 | tf_op jit(solution)/shard_map/psum | solution.py:48
  184.6 74.6 %psum.255 = f32[32,32]{0,1:T(8,128)S(1)} all-reduce(f32[32,32]{0,1:T(8,128)S(1)} %convolution_bitcast_fusion.11), channel_id=1, replica_groups=mesh['pr'=16,'pc'=8] {'pr'}, use_global_device_ids=true, to_apply=%region_3.4 | all-reduce | flops 1024 | bytes 8192 | tf_op jit(solution)/shard_map/psum | solution.py:49
  262.5 13.5 all-gather.2
  276.3 65.5 %all-reduce.43.cloned.1.call-done = (f32[32,1280]{1,0:T(8,128)}, f32[32,1280]{1,0:T(8,128)}, f32[32,1280]{1,0:T(8,128)}, f32[32,1280]{1,0:T(8,128)}) async-done(((f32[32,1280]{1,0:T(8,128)}, f32[32,1280]{1,0:T(8,128)}, f32[32,1280]{1,0:T(8,128)}, f32[32,1280]{1,0:T(8,128)}), (f32[32,1280]{1,0:T(8,128)}, f32[32,1280]{1,0:T(8,128)}, f32[32,1280]{1,0:T(8,128)}, ...) | async-done | bytes 655376 | tf_op jit(solution)/shard_map/psum | solution.py:9
  343.7 14.6 convolution_subtract_fusion.5
  376.5 56.5 %all-reduce.23.cloned.1.call-done = f32[32,1280]{1,0:T(8,128)} async-done(((f32[32,1280]{1,0:T(8,128)}), f32[32,1280]{1,0:T(8,128)}) %all-reduce.23.cloned.1.call-update) | async-done | bytes 163856 | tf_op jit(solution)/shard_map/psum | solution.py:48
  434.4 74.6 %psum.261 = f32[32,32]{0,1:T(8,128)S(1)} all-reduce(f32[32,32]{0,1:T(8,128)S(1)} %convolution_bitcast_fusion.10), channel_id=1, replica_groups=mesh['pr'=16,'pc'=8] {'pr'}, use_global_device_ids=true, to_apply=%region_9.10 | all-reduce | flops 1024 | bytes 8192 | tf_op jit(solution)/shard_map/psum | solution.py:49
  512.2 13.2 all-gather.3
  537.6 54.1 %all-reduce.41.cloned.1.call-done = (f32[32,1280]{1,0:T(8,128)}, f32[32,1280]{1,0:T(8,128)}, f32[32,1280]{1,0:T(8,128)}, f32[32,1280]{1,0:T(8,128)}) async-done(((f32[32,1280]{1,0:T(8,128)}, f32[32,1280]{1,0:T(8,128)}, f32[32,1280]{1,0:T(8,128)}, f32[32,1280]{1,0:T(8,128)}), (f32[32,1280]{1,0:T(8,128)}, f32[32,1280]{1,0:T(8,128)}, f32[32,1280]{1,0:T(8,128)}, ...) | async-done | bytes 655376 | tf_op jit(solution)/shard_map/psum | solution.py:9
  593.5 14.2 convolution_subtract_fusion.4
  626.0 56.5 %all-reduce.25.cloned.1.call-done = f32[32,1280]{1,0:T(8,128)} async-done(((f32[32,1280]{1,0:T(8,128)}), f32[32,1280]{1,0:T(8,128)}) %all-reduce.25.cloned.1.call-update) | async-done | bytes 163856 | tf_op jit(solution)/shard_map/psum | solution.py:48
  683.9 74.6 %psum.267 = f32[32,32]{0,1:T(8,128)S(1)} all-reduce(f32[32,32]{0,1:T(8,128)S(1)} %convolution_bitcast_fusion.9), channel_id=1, replica_groups=mesh['pr'=16,'pc'=8] {'pr'}, use_global_device_ids=true, to_apply=%region_15.16 | all-reduce | flops 1024 | bytes 8192 | tf_op jit(solution)/shard_map/psum | solution.py:49
  761.8 13.2 all-gather.4
  775.7 65.4 %all-reduce.39.cloned.1.call-done = (f32[32,1280]{1,0:T(8,128)}, f32[32,1280]{1,0:T(8,128)}, f32[32,1280]{1,0:T(8,128)}, f32[32,1280]{1,0:T(8,128)}) async-done(((f32[32,1280]{1,0:T(8,128)}, f32[32,1280]{1,0:T(8,128)}, f32[32,1280]{1,0:T(8,128)}, f32[32,1280]{1,0:T(8,128)}), (f32[32,1280]{1,0:T(8,128)}, f32[32,1280]{1,0:T(8,128)}, f32[32,1280]{1,0:T(8,128)}, ...) | async-done | bytes 655376 | tf_op jit(solution)/shard_map/psum | solution.py:9
  843.0 14.2 convolution_subtract_fusion.3
  875.5 56.5 %all-reduce.27.cloned.1.call-done = f32[32,1280]{1,0:T(8,128)} async-done(((f32[32,1280]{1,0:T(8,128)}), f32[32,1280]{1,0:T(8,128)}) %all-reduce.27.cloned.1.call-update) | async-done | bytes 163856 | tf_op jit(solution)/shard_map/psum | solution.py:48
  933.4 74.6 %psum.273 = f32[32,32]{0,1:T(8,128)S(1)} all-reduce(f32[32,32]{0,1:T(8,128)S(1)} %convolution_bitcast_fusion.8), channel_id=1, replica_groups=mesh['pr'=16,'pc'=8] {'pr'}, use_global_device_ids=true, to_apply=%region_21.22 | all-reduce | flops 1024 | bytes 8192 | tf_op jit(solution)/shard_map/psum | solution.py:49
  1011.2 13.2 all-gather.5
  1025.0 65.7 %all-reduce.37.cloned.1.call-done = (f32[32,1280]{1,0:T(8,128)}, f32[32,1280]{1,0:T(8,128)}, f32[32,1280]{1,0:T(8,128)}, f32[32,1280]{1,0:T(8,128)}) async-done(((f32[32,1280]{1,0:T(8,128)}, f32[32,1280]{1,0:T(8,128)}, f32[32,1280]{1,0:T(8,128)}, f32[32,1280]{1,0:T(8,128)}), (f32[32,1280]{1,0:T(8,128)}, f32[32,1280]{1,0:T(8,128)}, f32[32,1280]{1,0:T(8,128)}, ...) | async-done | bytes 655376 | tf_op jit(solution)/shard_map/psum | solution.py:9
  1092.5 14.2 convolution_subtract_fusion.2
  1125.0 56.5 %all-reduce.29.cloned.1.call-done = f32[32,1280]{1,0:T(8,128)} async-done(((f32[32,1280]{1,0:T(8,128)}), f32[32,1280]{1,0:T(8,128)}) %all-reduce.29.cloned.1.call-update) | async-done | bytes 163856 | tf_op jit(solution)/shard_map/psum | solution.py:48
  1182.9 74.6 %psum.279 = f32[32,32]{0,1:T(8,128)S(1)} all-reduce(f32[32,32]{0,1:T(8,128)S(1)} %convolution_bitcast_fusion.7), channel_id=1, replica_groups=mesh['pr'=16,'pc'=8] {'pr'}, use_global_device_ids=true, to_apply=%region_27.28 | all-reduce | flops 1024 | bytes 8192 | tf_op jit(solution)/shard_map/psum | solution.py:49
  1260.8 79.3 %all-reduce.35.cloned.1.call-done = (f32[32,1280]{1,0:T(8,128)}, f32[32,1280]{1,0:T(8,128)}, f32[32,1280]{1,0:T(8,128)}, f32[32,1280]{1,0:T(8,128)}) async-done(((f32[32,1280]{1,0:T(8,128)}, f32[32,1280]{1,0:T(8,128)}, f32[32,1280]{1,0:T(8,128)}, f32[32,1280]{1,0:T(8,128)}), (f32[32,1280]{1,0:T(8,128)}, f32[32,1280]{1,0:T(8,128)}, f32[32,1280]{1,0:T(8,128)}, ...) | async-done | bytes 655376 | tf_op jit(solution)/shard_map/psum | solution.py:9
  1342.0 14.4 convolution_subtract_fusion.1
  1374.0 57.2 %all-reduce.31.cloned.1.call-done = f32[32,1280]{1,0:T(8,128)} async-done(((f32[32,1280]{1,0:T(8,128)}), f32[32,1280]{1,0:T(8,128)}) %all-reduce.31.cloned.1.call-update) | async-done | bytes 163856 | tf_op jit(solution)/shard_map/psum | solution.py:48
  1432.5 74.9 %psum.285 = f32[32,32]{0,1:T(8,128)S(1)} all-reduce(f32[32,32]{0,1:T(8,128)S(1)} %convolution_bitcast_fusion.6), channel_id=1, replica_groups=mesh['pr'=16,'pc'=8] {'pr'}, use_global_device_ids=true, to_apply=%region_33.34 | all-reduce | flops 1024 | bytes 8192 | tf_op jit(solution)/shard_map/psum | solution.py:49
  1510.9 77.3 %all-reduce.33.cloned.1.call-done = (f32[32,1280]{1,0:T(8,128)}, f32[32,1280]{1,0:T(8,128)}) async-done(((f32[32,1280]{1,0:T(8,128)}, f32[32,1280]{1,0:T(8,128)}), (f32[32,1280]{1,0:T(8,128)}, f32[32,1280]{1,0:T(8,128)})) %all-reduce.33.cloned.1.call-update) | async-done | bytes 327696 | tf_op jit(solution)/shard_map/psum | solution.py:9
  1588.1 15.4 convolution_subtract_fusion
  (112 shorter events, 146.5 us)
Async XLA Ops:
  7.2 252.0 %copy-start.5 = (f32[6,32,32]{2,1,0:T(8,128)S(1)}, f32[6,32,32]{2,1,0:T(8,128)}, u32[]{:S(2)}) copy-start(f32[6,32,32]{2,1,0:T(8,128)} %param.5) | copy-start | bytes 73732
  7.2 101.6 %all-reduce.45.cloned.1.call-start = ((), (), s32[]{:S(2)}) async-start(), calls=%async_computation.12 | async-start | bytes 655360 | tf_op jit(solution)/shard_map/psum | solution.py:9
  23.2 160.1 %all-reduce.21.cloned.1.call-start = ((), (), s32[]{:S(2)}) async-start(), calls=%async_computation | async-start | bytes 327680 | tf_op jit(solution)/shard_map/psum | solution.py:48
  126.0 215.9 %all-reduce.43.cloned.1.call-start = ((), (), s32[]{:S(2)}) async-start(), calls=%async_computation.11 | async-start | bytes 1310720 | tf_op jit(solution)/shard_map/psum | solution.py:9
  262.4 170.6 %all-reduce.23.cloned.1.call-start = ((), (), s32[]{:S(2)}) async-start(), calls=%async_computation.1 | async-start | bytes 327680 | tf_op jit(solution)/shard_map/psum | solution.py:48
  358.3 5.0 copy-start.3
  375.7 216.0 %all-reduce.41.cloned.1.call-start = ((), (), s32[]{:S(2)}) async-start(), calls=%async_computation.10 | async-start | bytes 1310720 | tf_op jit(solution)/shard_map/psum | solution.py:9
  512.1 170.4 %all-reduce.25.cloned.1.call-start = ((), (), s32[]{:S(2)}) async-start(), calls=%async_computation.2 | async-start | bytes 327680 | tf_op jit(solution)/shard_map/psum | solution.py:48
  607.8 5.0 copy-start.2
  625.2 215.9 %all-reduce.39.cloned.1.call-start = ((), (), s32[]{:S(2)}) async-start(), calls=%async_computation.9 | async-start | bytes 1310720 | tf_op jit(solution)/shard_map/psum | solution.py:9
  761.6 170.4 %all-reduce.27.cloned.1.call-start = ((), (), s32[]{:S(2)}) async-start(), calls=%async_computation.3 | async-start | bytes 327680 | tf_op jit(solution)/shard_map/psum | solution.py:48
  857.3 5.0 copy-start.1
  874.7 216.0 %all-reduce.37.cloned.1.call-start = ((), (), s32[]{:S(2)}) async-start(), calls=%async_computation.8 | async-start | bytes 1310720 | tf_op jit(solution)/shard_map/psum | solution.py:9
  1011.1 170.4 %all-reduce.29.cloned.1.call-start = ((), (), s32[]{:S(2)}) async-start(), calls=%async_computation.4 | async-start | bytes 327680 | tf_op jit(solution)/shard_map/psum | solution.py:48
  1106.8 5.0 copy-start
  1124.2 215.9 %all-reduce.35.cloned.1.call-start = ((), (), s32[]{:S(2)}) async-start(), calls=%async_computation.7 | async-start | bytes 1310720 | tf_op jit(solution)/shard_map/psum | solution.py:9
  1260.6 170.6 %all-reduce.31.cloned.1.call-start = ((), (), s32[]{:S(2)}) async-start(), calls=%async_computation.5 | async-start | bytes 327680 | tf_op jit(solution)/shard_map/psum | solution.py:48
  1356.5 5.0 copy-start.4
  1373.9 214.3 %all-reduce.33.cloned.1.call-start = ((), (), s32[]{:S(2)}) async-start(), calls=%async_computation.6 | async-start | bytes 655360 | tf_op jit(solution)/shard_map/psum | solution.py:9
  1510.9 92.7 %copy-start.6 = (f32[6,32,160]{2,1,0:T(8,128)}, f32[6,32,160]{2,1,0:T(8,128)S(1)}, u32[]{:S(2)}) copy-start(f32[6,32,160]{2,1,0:T(8,128)S(1)} %constant_dynamic-update-slice_fusion.12) | copy-start | bytes 368644
Sparse Core Ops, SparseCore 0:
  23.3 85.4 all-reduce.44
  126.1 57.1 all-reduce.20
  262.5 79.3 all-reduce.42
  375.8 57.1 all-reduce.22
  512.2 79.4 all-reduce.40
  625.3 57.1 all-reduce.24
  761.7 79.3 all-reduce.38
  874.8 57.1 all-reduce.26
  1011.2 79.4 all-reduce.36
  1124.3 57.1 all-reduce.28
  1260.7 79.3 all-reduce.34
  1374.0 57.1 all-reduce.30
  1510.7 77.3 all-reduce.32
where the time goes:
time: 1620 us; the launch traced here: 1610 us
  waiting for transfers between devices  819 us (51%)
  blocking collectives  528 us (33%)
  matrix products  192 us (12%)
  local copies, waits for them, and re-layouts  52.1 us (3%)
    psum x7, waiting for transfers between devices, broadcast(): return lax.psum(kept, axis)  479 us
    psum x6, blocking collectives, per_device(): gram_block = lax.psum(contract(v_row, x_row, 1, 1), 'pr')  448 us
    psum x6, waiting for transfers between devices, per_device(): x_row = lax.psum(partial_value, 'pc')  340 us
    dot_general x42, matrix products, contract(): lax.dot_general(left_side, right_side, (((left_dim,), (right_dim,)), ((),...  192 us
    all_gather x6, blocking collectives, per_device(): v_row = lax.all_gather(v_panels[panel], 'pc', axis=1, tiled=True)  80.3 us
  transfers between devices with their start and end apart: 13, of which 13 were waited for; matrix products, arithmetic and copies ran while one was open for 1% of the time, Pallas kernels for 0%

commit v1 on v0

--- a/solution.py
+++ b/solution.py
@@ -1,7 +1,26 @@
+import functools
 import jax
 import jax.numpy as jnp
 from jax import lax
 from jax.sharding import PartitionSpec as P
+
+
+def map_the_hubs(arr_in, which_dim):
+    n_axis = lax.axis_size("pc")
+    near = sorted(((dev_i, (dev_i + 1) % n_axis) for dev_i in range(n_axis)))
+    carry_out = arr_in
+    sheets = [carry_out]
+    for kk in range(1, n_axis):
+        carry_out = lax.ppermute(carry_out, "pc", near)
+        sheets.insert(0, carry_out)
+    earlier = jnp.concatenate(sheets, axis=which_dim)
+    f_now = lax.axis_index("pc")
+    y1 = f_now + 1
+    part_next = jnp.roll(earlier, shift=y1 * arr_in.shape[which_dim], axis=which_dim)
+    return part_next
+
+
+raise_edges_all = functools.partial(map_the_hubs, which_dim=1)
 
 
 def broadcast(value, axis, source):
@@ -41,7 +60,7 @@
     share = rows_here // lax.axis_size("pc")
     w_blocks = []
     for panel in range(v_panels.shape[0]):
-        v_row = lax.all_gather(v_panels[panel], "pc", axis=1, tiled=True)
+        v_row = raise_edges_all(v_panels[panel])
         v_col = fetch_v_columns(v_row, col_rank, ratio)
         factor = t_panels[panel]
         partial_value = contract(v_col, matrix, 1, 1)

time: 1620 us -> 1640 us (1.012)
  waiting for transfers between devices: 819 us -> 925 us
  blocking collectives: 528 us -> 448 us
    ppermute x0 -> x42, waiting for transfers between devices: none -> 177 us  [map_the_hubs(): carry_out = lax.ppermute(carry_out, 'pc', near)]
    all_gather x6 -> x0, blocking collectives: 80.3 us -> none  [per_device(): v_row = lax.all_gather(v_panels[panel], 'pc', axis=1, tiled=True)]
    psum x7, waiting for transfers between devices: 479 us -> 407 us  [broadcast(): return lax.psum(kept, axis)]
  transfers between devices with their start and end apart: 13 -> 55, of which waited for: 13 -> 54; matrix products, arithmetic and copies ran while one was open for 1% -> 1% of each run, Pallas kernels for 0% -> 0%
where the time goes in v1:
time: 1640 us
  waiting for transfers between devices  925 us (56%)
  blocking collectives  448 us (27%)
  matrix products  201 us (12%)
  local copies, waits for them, and re-layouts  38 us (2%)
    psum x6, blocking collectives, per_device(): gram_block = lax.psum(contract(v_row, x_row, 1, 1), 'pr')  448 us
    psum x7, waiting for transfers between devices, broadcast(): return lax.psum(kept, axis)  407 us
    psum x6, waiting for transfers between devices, per_device(): x_row = lax.psum(partial_value, 'pc')  340 us
    dot_general x42, matrix products, contract(): lax.dot_general(left_side, right_side, (((left_dim,), (right_dim,)), ((),...  201 us
    ppermute x42, waiting for transfers between devices, map_the_hubs(): carry_out = lax.ppermute(carry_out, 'pc', near)  177 us
  transfers between devices with their start and end apart: 55, of which 54 were waited for; matrix products, arithmetic and copies ran while one was open for 1% of the time, Pallas kernels for 0%

profile of v1, /device:TPU:0, one launch (start us, length us, event | category | flops | bytes accessed | tf_op | source)
XLA Modules:
  0.0 1635.8 jit_solution(17727349386555279008)
XLA Ops:
  60.9 64.4 %all-reduce.45.cloned.1.call-done = (f32[32,1280]{1,0:T(8,128)}, f32[32,1280]{1,0:T(8,128)}) async-done(((f32[32,1280]{1,0:T(8,128)}, f32[32,1280]{1,0:T(8,128)}), (f32[32,1280]{1,0:T(8,128)}, f32[32,1280]{1,0:T(8,128)})) %all-reduce.45.cloned.1.call-update) | async-done | bytes 327696 | tf_op jit(solution)/shard_map/psum | solution.py:28
  127.2 15.3 fusion.120
  143.3 56.5 %all-reduce.21.cloned.1.call-done = f32[32,1280]{1,0:T(8,128)} async-done(((f32[32,1280]{1,0:T(8,128)}), f32[32,1280]{1,0:T(8,128)}) %all-reduce.21.cloned.1.call-update) | async-done | bytes 163856 | tf_op jit(solution)/shard_map/psum | solution.py:67
  201.0 74.6 %psum.255 = f32[32,32]{1,0:T(8,128)S(1)} all-reduce(f32[32,32]{1,0:T(8,128)S(1)} %fusion.121), channel_id=1, replica_groups=mesh['pr'=16,'pc'=8] {'pr'}, use_global_device_ids=true, to_apply=%region_3.5 | all-reduce | flops 1024 | bytes 8192 | tf_op jit(solution)/shard_map/psum | solution.py:68
  311.4 46.4 %all-reduce.43.cloned.1.call-done = (f32[32,1280]{1,0:T(8,128)}, f32[32,1280]{1,0:T(8,128)}, f32[32,1280]{1,0:T(8,128)}, f32[32,1280]{1,0:T(8,128)}) async-done(((f32[32,1280]{1,0:T(8,128)}, f32[32,1280]{1,0:T(8,128)}, f32[32,1280]{1,0:T(8,128)}, f32[32,1280]{1,0:T(8,128)}), (f32[32,1280]{1,0:T(8,128)}, f32[32,1280]{1,0:T(8,128)}, f32[32,1280]{1,0:T(8,128)}, ...) | async-done | bytes 655376 | tf_op jit(solution)/shard_map/psum | solution.py:28
  359.7 14.6 convolution_subtract_fusion.5
  374.3 4.9 copy-done.2
  379.2 12.4 fusion.122
  392.4 56.6 %all-reduce.23.cloned.1.call-done = f32[32,1280]{1,0:T(8,128)} async-done(((f32[32,1280]{1,0:T(8,128)}), f32[32,1280]{1,0:T(8,128)}) %all-reduce.23.cloned.1.call-update) | async-done | bytes 163856 | tf_op jit(solution)/shard_map/psum | solution.py:67
  450.2 74.6 %psum.261 = f32[32,32]{1,0:T(8,128)S(1)} all-reduce(f32[32,32]{1,0:T(8,128)S(1)} %fusion.123), channel_id=1, replica_groups=mesh['pr'=16,'pc'=8] {'pr'}, use_global_device_ids=true, to_apply=%region_9.11 | all-reduce | flops 1024 | bytes 8192 | tf_op jit(solution)/shard_map/psum | solution.py:68
  560.4 46.6 %all-reduce.41.cloned.1.call-done = (f32[32,1280]{1,0:T(8,128)}, f32[32,1280]{1,0:T(8,128)}, f32[32,1280]{1,0:T(8,128)}, f32[32,1280]{1,0:T(8,128)}) async-done(((f32[32,1280]{1,0:T(8,128)}, f32[32,1280]{1,0:T(8,128)}, f32[32,1280]{1,0:T(8,128)}, f32[32,1280]{1,0:T(8,128)}), (f32[32,1280]{1,0:T(8,128)}, f32[32,1280]{1,0:T(8,128)}, f32[32,1280]{1,0:T(8,128)}, ...) | async-done | bytes 655376 | tf_op jit(solution)/shard_map/psum | solution.py:28
  608.9 25.8 %convolution_subtract_fusion.4 = f32[1280,2560]{1,0:T(8,128)S(1)} fusion(f32[1280,2560]{1,0:T(8,128)} %copy-done.2, f32[32,2560]{1,0:T(8,128)S(1)} %constant_dynamic-update-slice_fusion.2, f32[32,1280]{1,0:T(8,128)} %get-tuple-element.17, f32[32,1280]{1,0:T(8,128)} %get-tuple-element.18, f32[32,1280]{1,0:T(8,128)S(1)} %get-tuple-element.58, ...), kind=kOutput, calls=%fused_computation.4 | convolution fusion | flops 2520268800 | bytes 27197440 | tf_op jit(solution)/shard_map/dot_general | solution.py:32
  639.6 12.4 fusion.124
  652.8 56.6 %all-reduce.25.cloned.1.call-done = f32[32,1280]{1,0:T(8,128)} async-done(((f32[32,1280]{1,0:T(8,128)}), f32[32,1280]{1,0:T(8,128)}) %all-reduce.25.cloned.1.call-update) | async-done | bytes 163856 | tf_op jit(solution)/shard_map/psum | solution.py:67
  710.6 74.6 %psum.267 = f32[32,32]{1,0:T(8,128)S(1)} all-reduce(f32[32,32]{1,0:T(8,128)S(1)} %fusion.125), channel_id=1, replica_groups=mesh['pr'=16,'pc'=8] {'pr'}, use_global_device_ids=true, to_apply=%region_15.17 | all-reduce | flops 1024 | bytes 8192 | tf_op jit(solution)/shard_map/psum | solution.py:68
  820.8 46.7 %all-reduce.39.cloned.1.call-done = (f32[32,1280]{1,0:T(8,128)}, f32[32,1280]{1,0:T(8,128)}, f32[32,1280]{1,0:T(8,128)}, f32[32,1280]{1,0:T(8,128)}) async-done(((f32[32,1280]{1,0:T(8,128)}, f32[32,1280]{1,0:T(8,128)}, f32[32,1280]{1,0:T(8,128)}, f32[32,1280]{1,0:T(8,128)}), (f32[32,1280]{1,0:T(8,128)}, f32[32,1280]{1,0:T(8,128)}, f32[32,1280]{1,0:T(8,128)}, ...) | async-done | bytes 655376 | tf_op jit(solution)/shard_map/psum | solution.py:28
  869.4 14.7 convolution_subtract_fusion.3
  889.0 12.4 fusion.126
  902.2 56.6 %all-reduce.27.cloned.1.call-done = f32[32,1280]{1,0:T(8,128)} async-done(((f32[32,1280]{1,0:T(8,128)}), f32[32,1280]{1,0:T(8,128)}) %all-reduce.27.cloned.1.call-update) | async-done | bytes 163856 | tf_op jit(solution)/shard_map/psum | solution.py:67
  959.9 74.6 %psum.273 = f32[32,32]{1,0:T(8,128)S(1)} all-reduce(f32[32,32]{1,0:T(8,128)S(1)} %fusion.127), channel_id=1, replica_groups=mesh['pr'=16,'pc'=8] {'pr'}, use_global_device_ids=true, to_apply=%region_21.23 | all-reduce | flops 1024 | bytes 8192 | tf_op jit(solution)/shard_map/psum | solution.py:68
  1070.2 46.6 %all-reduce.37.cloned.1.call-done = (f32[32,1280]{1,0:T(8,128)}, f32[32,1280]{1,0:T(8,128)}, f32[32,1280]{1,0:T(8,128)}, f32[32,1280]{1,0:T(8,128)}) async-done(((f32[32,1280]{1,0:T(8,128)}, f32[32,1280]{1,0:T(8,128)}, f32[32,1280]{1,0:T(8,128)}, f32[32,1280]{1,0:T(8,128)}), (f32[32,1280]{1,0:T(8,128)}, f32[32,1280]{1,0:T(8,128)}, f32[32,1280]{1,0:T(8,128)}, ...) | async-done | bytes 655376 | tf_op jit(solution)/shard_map/psum | solution.py:28
  1118.7 14.4 convolution_subtract_fusion.2
  1138.0 12.4 fusion.128
  1151.2 56.6 %all-reduce.29.cloned.1.call-done = f32[32,1280]{1,0:T(8,128)} async-done(((f32[32,1280]{1,0:T(8,128)}), f32[32,1280]{1,0:T(8,128)}) %all-reduce.29.cloned.1.call-update) | async-done | bytes 163856 | tf_op jit(solution)/shard_map/psum | solution.py:67
  1209.0 74.6 %psum.279 = f32[32,32]{1,0:T(8,128)S(1)} all-reduce(f32[32,32]{1,0:T(8,128)S(1)} %fusion.129), channel_id=1, replica_groups=mesh['pr'=16,'pc'=8] {'pr'}, use_global_device_ids=true, to_apply=%region_27.29 | all-reduce | flops 1024 | bytes 8192 | tf_op jit(solution)/shard_map/psum | solution.py:68
  1286.6 79.4 %all-reduce.35.cloned.1.call-done = (f32[32,1280]{1,0:T(8,128)}, f32[32,1280]{1,0:T(8,128)}, f32[32,1280]{1,0:T(8,128)}, f32[32,1280]{1,0:T(8,128)}) async-done(((f32[32,1280]{1,0:T(8,128)}, f32[32,1280]{1,0:T(8,128)}, f32[32,1280]{1,0:T(8,128)}, f32[32,1280]{1,0:T(8,128)}), (f32[32,1280]{1,0:T(8,128)}, f32[32,1280]{1,0:T(8,128)}, f32[32,1280]{1,0:T(8,128)}, ...) | async-done | bytes 655376 | tf_op jit(solution)/shard_map/psum | solution.py:28
  1367.8 14.5 convolution_subtract_fusion.1
  1387.2 12.4 fusion.130
  1399.8 57.2 %all-reduce.31.cloned.1.call-done = f32[32,1280]{1,0:T(8,128)} async-done(((f32[32,1280]{1,0:T(8,128)}), f32[32,1280]{1,0:T(8,128)}) %all-reduce.31.cloned.1.call-update) | async-done | bytes 163856 | tf_op jit(solution)/shard_map/psum | solution.py:67
  1458.2 74.9 %psum.285 = f32[32,32]{1,0:T(8,128)S(1)} all-reduce(f32[32,32]{1,0:T(8,128)S(1)} %fusion.131), channel_id=1, replica_groups=mesh['pr'=16,'pc'=8] {'pr'}, use_global_device_ids=true, to_apply=%region_33.35 | all-reduce | flops 1024 | bytes 8192 | tf_op jit(solution)/shard_map/psum | solution.py:68
  1536.1 77.3 %all-reduce.33.cloned.1.call-done = (f32[32,1280]{1,0:T(8,128)}, f32[32,1280]{1,0:T(8,128)}) async-done(((f32[32,1280]{1,0:T(8,128)}, f32[32,1280]{1,0:T(8,128)}), (f32[32,1280]{1,0:T(8,128)}, f32[32,1280]{1,0:T(8,128)})) %all-reduce.33.cloned.1.call-update) | async-done | bytes 327696 | tf_op jit(solution)/shard_map/psum | solution.py:28
  1613.4 15.4 convolution_subtract_fusion
  (190 shorter events, 244.3 us)
Async XLA Ops:
  7.2 118.1 %all-reduce.45.cloned.1.call-start = ((), (), s32[]{:S(2)}) async-start(), calls=%async_computation.12 | async-start | bytes 655360 | tf_op jit(solution)/shard_map/psum | solution.py:28
  8.1 4.6 collective-permute-start
  12.6 4.6 collective-permute-start.1
  17.2 4.6 collective-permute-start.2
  26.3 4.9 collective-permute-start.7
  30.8 4.6 collective-permute-start.5
  35.7 5.9 collective-permute-start.9
  41.6 158.1 %all-reduce.21.cloned.1.call-start = ((), (), s32[]{:S(2)}) async-start(), calls=%async_computation | async-start | bytes 327680 | tf_op jit(solution)/shard_map/psum | solution.py:67
  41.7 4.6 collective-permute-start.10
  50.8 4.6 collective-permute-start.12
  142.5 215.3 %all-reduce.43.cloned.1.call-start = ((), (), s32[]{:S(2)}) async-start(), calls=%async_computation.11 | async-start | bytes 1310720 | tf_op jit(solution)/shard_map/psum | solution.py:28
  278.3 170.7 %all-reduce.23.cloned.1.call-start = ((), (), s32[]{:S(2)}) async-start(), calls=%async_computation.1 | async-start | bytes 327680 | tf_op jit(solution)/shard_map/psum | solution.py:67
  278.6 4.6 collective-permute-start.14
  292.2 4.6 collective-permute-start.17
  305.9 4.6 collective-permute-start.20
  391.7 215.3 %all-reduce.41.cloned.1.call-start = ((), (), s32[]{:S(2)}) async-start(), calls=%async_computation.10 | async-start | bytes 1310720 | tf_op jit(solution)/shard_map/psum | solution.py:28
  527.5 181.9 %all-reduce.25.cloned.1.call-start = ((), (), s32[]{:S(2)}) async-start(), calls=%async_computation.2 | async-start | bytes 327680 | tf_op jit(solution)/shard_map/psum | solution.py:67
  527.6 4.6 collective-permute-start.21
  536.7 4.6 collective-permute-start.23
  652.1 215.4 %all-reduce.39.cloned.1.call-start = ((), (), s32[]{:S(2)}) async-start(), calls=%async_computation.9 | async-start | bytes 1310720 | tf_op jit(solution)/shard_map/psum | solution.py:28
  787.9 170.8 %all-reduce.27.cloned.1.call-start = ((), (), s32[]{:S(2)}) async-start(), calls=%async_computation.3 | async-start | bytes 327680 | tf_op jit(solution)/shard_map/psum | solution.py:67
  788.0 4.6 collective-permute-start.28
  797.1 4.6 collective-permute-start.30
  810.8 4.6 collective-permute-start.33
  901.4 215.3 %all-reduce.37.cloned.1.call-start = ((), (), s32[]{:S(2)}) async-start(), calls=%async_computation.8 | async-start | bytes 1310720 | tf_op jit(solution)/shard_map/psum | solution.py:28
  1037.3 170.5 %all-reduce.29.cloned.1.call-start = ((), (), s32[]{:S(2)}) async-start(), calls=%async_computation.4 | async-start | bytes 327680 | tf_op jit(solution)/shard_map/psum | solution.py:67
  1037.3 4.6 collective-permute-start.35
  1041.9 4.6 collective-permute-start.36
  1055.6 4.6 collective-permute-start.39
  1150.5 215.4 %all-reduce.35.cloned.1.call-start = ((), (), s32[]{:S(2)}) async-start(), calls=%async_computation.7 | async-start | bytes 1310720 | tf_op jit(solution)/shard_map/psum | solution.py:28
  1286.4 170.6 %all-reduce.31.cloned.1.call-start = ((), (), s32[]{:S(2)}) async-start(), calls=%async_computation.5 | async-start | bytes 327680 | tf_op jit(solution)/shard_map/psum | solution.py:67
  1399.7 213.7 %all-reduce.33.cloned.1.call-start = ((), (), s32[]{:S(2)}) async-start(), calls=%async_computation.6 | async-start | bytes 655360 | tf_op jit(solution)/shard_map/psum | solution.py:28
  (30 other events, 490.5 us)
Sparse Core Ops, SparseCore 0:
  41.7 83.5 all-reduce.44
  142.6 57.0 all-reduce.20
  278.4 79.3 all-reduce.42
  391.8 57.1 all-reduce.22
  527.6 79.3 all-reduce.40
  652.2 57.1 all-reduce.24
  788.1 79.3 all-reduce.38
  901.6 57.1 all-reduce.26
  1037.4 79.3 all-reduce.36
  1150.6 57.1 all-reduce.28
  1286.5 79.3 all-reduce.34
  1399.8 57.1 all-reduce.30
  1536.0 77.3 all-reduce.32
